TPU v7x, 256 devices: a whole 4x4x8 slice. The times are simulated.
256 devices in a mesh: samp: 4 (over y), var: 64 (over z, x, core).
Axes of the slice: x: 4, y: 4, z: 8, core: 2. Of those that a mesh axis runs over, the one named last changes fastest.
Arguments:
- dosage: bfloat16 [8192, 131072], P('samp', 'var'), may hold values from -16 to 16
- traits: float32 [8192, 128], P(('samp', 'var')), may hold values from -6 to 6
- coef_now: float32 [1024, 256, 128], P('var', 'samp'), may hold values from -6 to 6
- coef_prev: float32 [1024, 256, 128], P('var', 'samp'), may hold values from -6 to 6
- block_inverse: bfloat16 [1024, 256, 4, 256], P('var', 'samp'), may hold values from -0.1875 to 0.1875
- penalty: float32 [128], replicated, may hold values from 0.05 to 0.5
- block_start: int32 [512], replicated, may hold values from 0 to 1, as said below
- unit_owner: int32 [512], replicated, may hold values from 0 to 63, as said below
Outputs:
- coef_next: float32 [1024, 256, 128], P('var', 'samp')
- residual: float32 [8192, 128], P(('samp', 'var'))
Inputs may be any that keep to these rules, and one draw needn't show every extreme that they name: `block_start`: 1 where a linkage block begins, else 0. The first unit of every device's 8 units begins a block, and a block holds 1 to 4 units of 256 variants. `unit_owner`: the index along var of the device that owns each unit's block, equal for all units of a block. For a unit of the device with index d along var it is (d + j) modulo the size of var, with 1 <= j <= 4. An owner holds at most 16 units and some owner holds exactly 16; the units of one device that belong to one owner are at most 4, and some device has exactly 4 for one owner.
All inputs are finite; a program needn't handle non-finite values.
Results may differ from a plain program's by a relative error of at most 0.0072.
Values may be sent and summed in bfloat16 or wider, within the bound.
A program may use at most 64 MiB of HBM per device.

v0:
```python
import math

import jax
import jax.numpy as jnp
from jax import lax
from jax.sharding import PartitionSpec as P

MOMENTA = (0.4, 0.55)


def shifted(block, axis, distance):
    devices = range(lax.axis_size(axis))
    route = [((i - distance) % len(devices), i) for i in devices]
    return lax.ppermute(block, axis, route)


def copy_for_each(value, axis):
    length = lax.axis_size(axis)
    return lax.all_to_all(
        jnp.broadcast_to(value[None], (length, *value.shape)), axis, 0, 0, tiled=True
    )


def joined_along(pieces, dim):
    shape = list(pieces.shape[1:])
    shape[dim] *= pieces.shape[0]
    return jnp.moveaxis(pieces, 0, dim).reshape(shape)


def collect(value, axis, dim):
    pieces = copy_for_each(value, axis)
    return joined_along(pieces, dim)


def in_blocks(value, dim, length):
    before, after = (value.shape[:dim], value.shape[dim + 1 :])
    return jnp.moveaxis(value.reshape(*before, length, -1, *after), dim, 0)


def summed_on_arrival(value, axis, dim):
    length = lax.axis_size(axis)
    pieces = lax.all_to_all(in_blocks(value, dim, length), axis, 0, 0, tiled=True)
    return jnp.sum(pieces, axis=0)


def unit_tables(block_start, unit_owner, per_device, owners):
    unit_count = block_start.shape[0]
    unit_ids = jnp.arange(unit_count, dtype=jnp.int32)
    shard_of = unit_ids // per_device
    owner_hot = (unit_owner[:, None] == jnp.arange(owners, dtype=jnp.int32)[None, :]).astype(
        jnp.int32
    )
    running = jnp.cumsum(owner_hot, axis=0) - owner_hot
    slot_index = jnp.sum(running * owner_hot, axis=1)
    first_unit = shard_of * per_device
    before_shard = jnp.sum(running[first_unit] * owner_hot, axis=1)
    pair_place = slot_index - before_shard
    block_begin = lax.cummax(jnp.where(block_start == 1, unit_ids, 0), axis=0)
    block_later = lax.cummin(
        jnp.where(block_start == 1, unit_ids, unit_count), axis=0, reverse=True
    )
    block_follow = jnp.concatenate([block_later[1:], jnp.full((1,), unit_count, jnp.int32)])
    block_length = block_follow - block_begin
    offset = unit_ids - block_begin
    return (shard_of, slot_index, pair_place, offset, block_length)


def shards(dosage, traits, coef_now, coef_prev, block_inverse, penalty, block_start, unit_owner):
    owners = lax.axis_size("var")
    quarters = lax.axis_size("samp")
    var_index = lax.axis_index("var")
    capacity = coef_now.shape[0]
    quarter_rows = coef_now.shape[1]
    right_cols = coef_now.shape[2]
    unit_rows = block_inverse.shape[3]
    block_most = block_inverse.shape[2]
    per_device = dosage.shape[1] // unit_rows
    pair_cap = min(block_most, per_device)
    reach = capacity // pair_cap
    samples = dosage.shape[0] * quarters
    variants = dosage.shape[1] * owners
    inv_scale = 1.0 / math.sqrt(variants)
    grad_scale = 0.5 / math.sqrt(samples)
    shard_of, slot_index, pair_place, offset, block_length = unit_tables(
        block_start, unit_owner, per_device, owners
    )
    owner_gap = (unit_owner - shard_of) % owners
    unit_code = (owner_gap - 1) * pair_cap + pair_place
    columns = jnp.arange(reach * pair_cap, dtype=jnp.int32)
    local_ids = var_index * per_device + jnp.arange(per_device, dtype=jnp.int32)
    local_code = unit_code[local_ids]
    matches = local_code[None, :] == columns[:, None]
    send_unit = jnp.sum(
        matches.astype(jnp.int32) * jnp.arange(per_device, dtype=jnp.int32)[None, :], axis=1
    )
    send_live = jnp.any(matches, axis=1)
    owned_flag = unit_owner == var_index
    slot_match = owned_flag[None, :] & (
        slot_index[None, :] == jnp.arange(capacity, dtype=jnp.int32)[:, None]
    )
    slot_hits = slot_match.astype(jnp.int32)
    slot_live = jnp.any(slot_match, axis=1)
    slot_code = jnp.sum(slot_hits * unit_code[None, :], axis=1)
    slot_offset = jnp.sum(slot_hits * offset[None, :], axis=1)
    slot_length = jnp.sum(slot_hits * block_length[None, :], axis=1)
    back_match = slot_live[None, :] & (slot_code[None, :] == columns[:, None])
    back_slot = jnp.sum(
        back_match.astype(jnp.int32) * jnp.arange(capacity, dtype=jnp.int32)[None, :], axis=1
    )
    back_live = jnp.any(back_match, axis=1)
    within = jnp.arange(block_most, dtype=jnp.int32)
    member_ids = jnp.clip(
        jnp.arange(capacity, dtype=jnp.int32)[:, None] - slot_offset[:, None] + within[None, :],
        0,
        capacity - 1,
    )
    member_live = (within[None, :] < slot_length[:, None]) & slot_live[:, None]
    panel_rows = block_inverse.reshape(capacity, quarter_rows, block_most * unit_rows)
    zero_half = jnp.zeros((), jnp.bfloat16)
    current, previous = (coef_now, coef_prev)
    residual = traits
    for momentum in MOMENTA:
        point = current + momentum * (current - previous)
        send_outgoing = jnp.where(
            back_live[:, None, None], point.astype(jnp.bfloat16)[back_slot], zero_half
        )
        send_outgoing = send_outgoing.reshape(reach, pair_cap, quarter_rows, right_cols)
        send_pieces = []
        for send_gap in range(1, reach + 1):
            send_pieces.append(shifted(send_outgoing[send_gap - 1], "var", -send_gap))
        send_received = jnp.stack(send_pieces).reshape(reach * pair_cap, quarter_rows, right_cols)
        local_rows = send_received[local_code]
        send_gathered = collect(local_rows[:, None], "samp", 1)
        values = send_gathered.reshape(per_device * unit_rows, right_cols)
        summed = summed_on_arrival(
            jnp.dot(dosage, values, preferred_element_type=jnp.float32) * inv_scale, "var", 0
        )
        residual = summed - traits
        residual_b = collect(residual.astype(jnp.bfloat16), "var", 0)
        partial_grad = (
            lax.dot_general(
                dosage, residual_b, (((0,), (0,)), ((), ())), preferred_element_type=jnp.float32
            )
            * grad_scale
        )
        shaped = partial_grad.reshape(per_device, quarters, quarter_rows, right_cols)
        own_grad = summed_on_arrival(shaped, "samp", 1)[:, 0]
        outgoing = jnp.where(
            send_live[:, None, None], own_grad.astype(jnp.bfloat16)[send_unit], zero_half
        )
        outgoing = outgoing.reshape(reach, pair_cap, quarter_rows, right_cols)
        pieces = []
        for gap in range(1, reach + 1):
            pieces.append(shifted(outgoing[gap - 1], "var", gap))
        received = jnp.stack(pieces).reshape(reach * pair_cap, quarter_rows, right_cols)
        held_rows = jnp.where(slot_live[:, None, None], received[slot_code], zero_half)
        gathered = collect(held_rows[:, None], "samp", 1)
        whole_grad = gathered.reshape(capacity, unit_rows, right_cols)
        block_grad = jnp.where(member_live[:, :, None, None], whole_grad[member_ids], zero_half)
        block_grad = block_grad.reshape(capacity, block_most * unit_rows, right_cols)
        direction = jnp.einsum(
            "irc,ick->irk", panel_rows, block_grad, preferred_element_type=jnp.float32
        )
        stepped = point - direction
        updated = jnp.sign(stepped) * jnp.maximum(jnp.abs(stepped) - penalty, 0.0)
        updated = jnp.where(slot_live[:, None, None], updated, jnp.float32(0.0))
        previous, current = (current, updated)
    return (current, residual)


def solution(mesh):
    placed = (
        P("samp", "var"),
        P(("samp", "var"), None),
        P("var", "samp", None),
        P("var", "samp", None),
        P("var", "samp", None, None),
        P(),
        P(),
        P(),
    )
    return jax.shard_map(
        shards,
        mesh=mesh,
        in_specs=placed,
        out_specs=(P("var", "samp", None), P(("samp", "var"), None)),
        check_vma=False,
    )
```

profile of v0, /device:TPU:1, one launch (start us, length us, event | category | flops | bytes accessed | tf_op | source)
XLA Modules:
  0.0 334.4 jit_solution(2613917532027763792)
XLA Ops:
  2.0 2.4 reduce-window.26
  6.0 1.2 reduce-window.24
  12.1 3.3 collective-permute-start
  15.4 6.3 %collective-permute-start.3 = (bf16[4,64,128]{2,1,0:T(8,128)(2,1)S(1)}, bf16[4,64,128]{2,1,0:T(8,128)(2,1)S(1)}, u32[]{:S(2)}, u32[]{:S(2)}) collective-permute-start(bf16[4,64,128]{2,1,0:T(8,128)(2,1)S(1)} %get-tuple-element.24), channel_id=1, source_target_pairs={{4,0},{5,1},{6,2},{7,3},{8,4},{9,5},{10,6},{11,7},{12,8},{13,9},{1... | collective-permute-start | bytes 196616 | tf_op jit(solution)/shard_map/ppermute | solution.py:14
  21.7 1.1 collective-permute-start.2
  22.8 2.2 collective-permute-start.1
  25.7 1.2 collective-permute-done.2
  27.7 12.5 %all_to_all.50 = bf16[4,8,1,64,128]{4,3,1,2,0:T(8,128)(2,1)S(1)} all-to-all(bf16[4,8,1,64,128]{4,3,1,2,0:T(8,128)(2,1)S(1)} %broadcast_in_dim.167), channel_id=1, replica_groups=mesh['samp'=4,'var'=64] {'samp'}, dimensions={0} | all-to-all | bytes 1048576 | tf_op jit(solution)/shard_map/all_to_all | solution.py:19
  40.2 6.3 %fusion.3 = f32[2048,128]{0,1:T(8,128)S(1)} fusion(bf16[2048,128]{1,0:T(8,128)(2,1)S(1)} %bitcast.130, bf16[2048,2048]{1,0:T(8,128)(2,1)} %param.8), kind=kOutput, calls=%fused_computation.21 | convolution fusion | flops 1074003968 | bytes 9961472 | tf_op jit(solution)/shard_map/dot_general | solution.py:136
  46.9 36.9 %all_to_all.51 = f32[64,32,128]{2,1,0:T(8,128)S(1)} all-to-all(f32[64,32,128]{2,1,0:T(8,128)S(1)} %bitcast.124), channel_id=1, replica_groups=mesh['samp'=4,'var'=64] {'var'}, dimensions={0} | all-to-all | bytes 2097152 | tf_op jit(solution)/shard_map/all_to_all | solution.py:42
  84.0 24.0 %all_to_all.52 = bf16[64,32,128]{2,1,0:T(8,128)(2,1)S(1)} all-to-all(bf16[64,32,128]{2,1,0:T(8,128)(2,1)S(1)} %broadcast_in_dim.168), channel_id=1, replica_groups=mesh['samp'=4,'var'=64] {'var'}, dimensions={0} | all-to-all | bytes 1048576 | tf_op jit(solution)/shard_map/all_to_all | solution.py:19
  108.0 4.7 %fusion.2 = f32[2048,128]{0,1:T(8,128)S(1)} fusion(bf16[2048,128]{1,0:T(8,128)(2,1)S(1)} %bitcast.128, bf16[2048,2048]{1,0:T(8,128)(2,1)} %param.8), kind=kOutput, calls=%fused_computation.19 | convolution fusion | flops 1074003968 | bytes 9961472 | tf_op jit(solution)/shard_map/dot_general | solution.py:141
  114.0 3.5 %all-to-all-start.3 = ((f32[4,8,1,64,128]{4,3,1,2,0:T(8,128)}), f32[4,8,1,64,128]{4,3,1,2,0:T(8,128)S(1)}, u32[]{:S(2)}, u32[]{:S(2)}) async-start(f32[4,8,1,64,128]{4,3,1,2,0:T(8,128)} %copy.33), calls=%async_computation.3 | async-start | bytes 2097152 | tf_op jit(solution)/shard_map/all_to_all | solution.py:42
  117.8 14.6 %all-to-all-done.3 = f32[4,8,1,64,128]{4,3,1,2,0:T(8,128)S(1)} async-done(((f32[4,8,1,64,128]{4,3,1,2,0:T(8,128)}), f32[4,8,1,64,128]{4,3,1,2,0:T(8,128)S(1)}, u32[]{:S(2)}, u32[]{:S(2)}) %all-to-all-start.3) | async-done | bytes 1048608 | tf_op jit(solution)/shard_map/all_to_all | solution.py:42
  133.2 2.3 collective-permute-start.4
  136.4 1.7 collective-permute-start.6
  138.1 1.2 collective-permute-start.5
  139.3 3.2 collective-permute-done.7
  142.5 1.9 collective-permute-done.6
  144.4 1.1 collective-permute-done.5
  146.2 1.3 broadcast_in_dim.169
  147.5 4.2 %all-to-all-start.4 = ((bf16[4,16,1,64,128]{4,3,1,2,0:T(8,128)(2,1)}), bf16[4,16,1,64,128]{4,3,1,2,0:T(8,128)(2,1)}, u32[]{:S(2)}, u32[]{:S(2)}) async-start(bf16[4,16,1,64,128]{4,3,1,2,0:T(8,128)(2,1)} %broadcast_in_dim.169), calls=%async_computation.4 | async-start | bytes 2097152 | tf_op jit(solution)/shard_map/all_to_all | solution.py:19
  152.1 3.2 reshape.391
  155.3 10.7 %all-to-all-done.4 = bf16[4,16,1,64,128]{4,3,1,2,0:T(8,128)(2,1)} async-done(((bf16[4,16,1,64,128]{4,3,1,2,0:T(8,128)(2,1)}), bf16[4,16,1,64,128]{4,3,1,2,0:T(8,128)(2,1)}, u32[]{:S(2)}, u32[]{:S(2)}) %all-to-all-start.4) | async-done | bytes 1048608 | tf_op jit(solution)/shard_map/all_to_all | solution.py:19
  166.1 1.3 copy.34
  167.4 3.0 gather_fusion.6
  170.4 6.2 %bitcast_select_fusion.1 = bf16[16,1024,128]{2,1,0:T(8,128)(2,1)S(1)} fusion(pred[16,1024]{1,0:T(8,128)(4,1)S(1)} %bitcast.136, bf16[16,1024,128]{2,1,0:T(8,128)(2,1)} %bitcast.123), kind=kLoop, calls=%fused_computation.13 | loop fusion | flops 2097152 | bytes 8404992 | tf_op jit(solution)/shard_map/jit(_where)/select_n | solution.py:159
  176.6 1.8 fusion.33
  179.1 1.8 collective-permute-start.8
  181.8 1.4 collective-permute-start.10
  184.1 2.1 collective-permute-done.11
  187.8 10.7 %all_to_all.53 = bf16[4,8,1,64,128]{4,3,1,2,0:T(8,128)(2,1)S(1)} all-to-all(bf16[4,8,1,64,128]{4,3,1,2,0:T(8,128)(2,1)S(1)} %broadcast_in_dim.171), channel_id=1, replica_groups=mesh['samp'=4,'var'=64] {'samp'}, dimensions={0} | all-to-all | bytes 1048576 | tf_op jit(solution)/shard_map/all_to_all | solution.py:19
  198.6 6.3 %fusion.1 = f32[2048,128]{0,1:T(8,128)S(1)} fusion(bf16[2048,128]{1,0:T(8,128)(2,1)S(1)} %bitcast.131, bf16[2048,2048]{1,0:T(8,128)(2,1)} %param.8), kind=kOutput, calls=%fused_computation.17 | convolution fusion | flops 1074003968 | bytes 9961472 | tf_op jit(solution)/shard_map/dot_general | solution.py:136
  204.9 1.3 copy.36
  206.2 37.1 %all_to_all.54 = f32[64,32,128]{2,1,0:T(8,128)S(1)} all-to-all(f32[64,32,128]{2,1,0:T(8,128)} %bitcast.126), channel_id=1, replica_groups=mesh['samp'=4,'var'=64] {'var'}, dimensions={0} | all-to-all | bytes 2097152 | tf_op jit(solution)/shard_map/all_to_all | solution.py:42
  244.1 24.0 %all_to_all.55 = bf16[64,32,128]{2,1,0:T(8,128)(2,1)S(1)} all-to-all(bf16[64,32,128]{2,1,0:T(8,128)(2,1)S(1)} %broadcast_in_dim.172), channel_id=1, replica_groups=mesh['samp'=4,'var'=64] {'var'}, dimensions={0} | all-to-all | bytes 1048576 | tf_op jit(solution)/shard_map/all_to_all | solution.py:19
  268.1 5.7 %fusion = f32[2048,128]{0,1:T(8,128)} fusion(bf16[2048,128]{1,0:T(8,128)(2,1)S(1)} %bitcast.129, bf16[2048,2048]{1,0:T(8,128)(2,1)} %param.8), kind=kOutput, calls=%fused_computation.15 | convolution fusion | flops 1074003968 | bytes 9961472 | tf_op jit(solution)/shard_map/dot_general | solution.py:141
  273.8 1.5 copy.37
  275.4 17.3 %all_to_all.56 = f32[4,8,1,64,128]{4,3,1,2,0:T(8,128)S(1)} all-to-all(f32[4,8,1,64,128]{4,3,1,2,0:T(8,128)S(1)} %copy.38), channel_id=1, replica_groups=mesh['samp'=4,'var'=64] {'samp'}, dimensions={0} | all-to-all | bytes 2097152 | tf_op jit(solution)/shard_map/all_to_all | solution.py:42
  293.5 2.3 collective-permute-start.12
  296.7 1.7 collective-permute-start.14
  298.4 1.2 collective-permute-start.13
  299.6 3.2 collective-permute-done.15
  302.8 1.9 collective-permute-done.14
  306.7 16.6 %all_to_all.57 = bf16[4,16,1,64,128]{4,3,1,2,0:T(8,128)(2,1)S(1)} all-to-all(bf16[4,16,1,64,128]{4,3,1,2,0:T(8,128)(2,1)S(1)} %broadcast_in_dim.173), channel_id=1, replica_groups=mesh['samp'=4,'var'=64] {'samp'}, dimensions={0} | all-to-all | bytes 2097152 | tf_op jit(solution)/shard_map/all_to_all | solution.py:19
  323.5 3.0 gather_fusion.11
  326.5 6.1 %bitcast_select_fusion = bf16[16,1024,128]{2,1,0:T(8,128)(2,1)S(1)} fusion(pred[16,1024]{1,0:T(8,128)(4,1)S(1)} %bitcast.137, bf16[16,1024,128]{2,1,0:T(8,128)(2,1)} %bitcast.122), kind=kLoop, calls=%fused_computation.12 | loop fusion | flops 2097152 | bytes 8404992 | tf_op jit(solution)/shard_map/jit(_where)/select_n | solution.py:159
  332.6 1.8 multiply_select_fusion
  (117 shorter events, 22.9 us)
Async XLA Ops:
  0.6 10.1 %copy-start.6 = (s32[512]{0:T(512)S(1)}, s32[512]{0:T(512)}, u32[]{:S(2)}) copy-start(s32[512]{0:T(512)} %param.15) | copy-start | bytes 6148
  0.6 10.6 %copy-start.2 = (f32[16,64,128]{2,1,0:T(8,128)S(1)}, f32[16,64,128]{2,1,0:T(8,128)}, u32[]{:S(2)}) copy-start(f32[16,64,128]{2,1,0:T(8,128)} %param.11) | copy-start | bytes 1572868
  0.7 10.6 %copy-start = (f32[16,64,128]{2,1,0:T(8,128)S(1)}, f32[16,64,128]{2,1,0:T(8,128)}, u32[]{:S(2)}) copy-start(f32[16,64,128]{2,1,0:T(8,128)} %param.10) | copy-start | bytes 1572868
  12.1 13.6 %collective-permute-start = (bf16[4,64,128]{2,1,0:T(8,128)(2,1)S(1)}, bf16[4,64,128]{2,1,0:T(8,128)(2,1)S(1)}, u32[]{:S(2)}, u32[]{:S(2)}) collective-permute-start(bf16[4,64,128]{2,1,0:T(8,128)(2,1)S(1)} %get-tuple-element.23), channel_id=1, source_target_pairs={{1,0},{2,1},{3,2},{4,3},{5,4},{6,5},{7,6},{8,7},{9,8},{10,9},{11,1... | collective-permute-start | bytes 196616 | tf_op jit(solution)/shard_map/ppermute | solution.py:14
  15.4 10.3 %collective-permute-start.3 = (bf16[4,64,128]{2,1,0:T(8,128)(2,1)S(1)}, bf16[4,64,128]{2,1,0:T(8,128)(2,1)S(1)}, u32[]{:S(2)}, u32[]{:S(2)}) collective-permute-start(bf16[4,64,128]{2,1,0:T(8,128)(2,1)S(1)} %get-tuple-element.24), channel_id=1, source_target_pairs={{4,0},{5,1},{6,2},{7,3},{8,4},{9,5},{10,6},{11,7},{12,8},{13,9},{1... | collective-permute-start | bytes 196616 | tf_op jit(solution)/shard_map/ppermute | solution.py:14
  21.7 5.2 %collective-permute-start.2 = (bf16[4,64,128]{2,1,0:T(8,128)(2,1)S(1)}, bf16[4,64,128]{2,1,0:T(8,128)(2,1)S(1)}, u32[]{:S(2)}, u32[]{:S(2)}) collective-permute-start(bf16[4,64,128]{2,1,0:T(8,128)(2,1)S(1)} %get-tuple-element.25), channel_id=1, source_target_pairs={{3,0},{4,1},{5,2},{6,3},{7,4},{8,5},{9,6},{10,7},{11,8},{12,9},{13... | collective-permute-start | bytes 196616 | tf_op jit(solution)/shard_map/ppermute | solution.py:14
  22.8 4.1 %collective-permute-start.1 = (bf16[4,64,128]{2,1,0:T(8,128)(2,1)S(1)}, bf16[4,64,128]{2,1,0:T(8,128)(2,1)S(1)}, u32[]{:S(2)}, u32[]{:S(2)}) collective-permute-start(bf16[4,64,128]{2,1,0:T(8,128)(2,1)S(1)} %get-tuple-element.26), channel_id=1, source_target_pairs={{2,0},{3,1},{4,2},{5,3},{6,4},{7,5},{8,6},{9,7},{10,8},{11,9},{12,... | collective-permute-start | bytes 196616 | tf_op jit(solution)/shard_map/ppermute | solution.py:14
  46.5 37.3 %copy-start.5 = (f32[32,128]{1,0:T(8,128)S(1)}, f32[32,128]{1,0:T(8,128)}, u32[]{:S(2)}) copy-start(f32[32,128]{1,0:T(8,128)} %param.9) | copy-start | bytes 49156
  114.0 18.3 %all-to-all-start.3 = ((f32[4,8,1,64,128]{4,3,1,2,0:T(8,128)}), f32[4,8,1,64,128]{4,3,1,2,0:T(8,128)S(1)}, u32[]{:S(2)}, u32[]{:S(2)}) async-start(f32[4,8,1,64,128]{4,3,1,2,0:T(8,128)} %copy.33), calls=%async_computation.3 | async-start | bytes 2097152 | tf_op jit(solution)/shard_map/all_to_all | solution.py:42
  133.2 6.1 %collective-permute-start.4 = (bf16[4,64,128]{2,1,0:T(8,128)(2,1)S(1)}, bf16[4,64,128]{2,1,0:T(8,128)(2,1)S(1)}, u32[]{:S(2)}, u32[]{:S(2)}) collective-permute-start(bf16[4,64,128]{2,1,0:T(8,128)(2,1)S(1)} %get-tuple-element.19), channel_id=1, source_target_pairs={{63,0},{0,1},{1,2},{2,3},{3,4},{4,5},{5,6},{6,7},{7,8},{8,9},{9,10... | collective-permute-start | bytes 196616 | tf_op jit(solution)/shard_map/ppermute | solution.py:14
  135.4 7.1 %collective-permute-start.7 = (bf16[4,64,128]{2,1,0:T(8,128)(2,1)S(1)}, bf16[4,64,128]{2,1,0:T(8,128)(2,1)S(1)}, u32[]{:S(2)}, u32[]{:S(2)}) collective-permute-start(bf16[4,64,128]{2,1,0:T(8,128)(2,1)S(1)} %get-tuple-element.20), channel_id=1, source_target_pairs={{60,0},{61,1},{62,2},{63,3},{0,4},{1,5},{2,6},{3,7},{4,8},{5,9},{6... | collective-permute-start | bytes 196616 | tf_op jit(solution)/shard_map/ppermute | solution.py:14
  136.4 7.9 %collective-permute-start.6 = (bf16[4,64,128]{2,1,0:T(8,128)(2,1)S(1)}, bf16[4,64,128]{2,1,0:T(8,128)(2,1)S(1)}, u32[]{:S(2)}, u32[]{:S(2)}) collective-permute-start(bf16[4,64,128]{2,1,0:T(8,128)(2,1)S(1)} %get-tuple-element.21), channel_id=1, source_target_pairs={{61,0},{62,1},{63,2},{0,3},{1,4},{2,5},{3,6},{4,7},{5,8},{6,9},{7,... | collective-permute-start | bytes 196616 | tf_op jit(solution)/shard_map/ppermute | solution.py:14
  138.1 7.3 %collective-permute-start.5 = (bf16[4,64,128]{2,1,0:T(8,128)(2,1)S(1)}, bf16[4,64,128]{2,1,0:T(8,128)(2,1)S(1)}, u32[]{:S(2)}, u32[]{:S(2)}) collective-permute-start(bf16[4,64,128]{2,1,0:T(8,128)(2,1)S(1)} %get-tuple-element.22), channel_id=1, source_target_pairs={{62,0},{63,1},{0,2},{1,3},{2,4},{3,5},{4,6},{5,7},{6,8},{7,9},{8,1... | collective-permute-start | bytes 196616 | tf_op jit(solution)/shard_map/ppermute | solution.py:14
  147.5 18.6 %all-to-all-start.4 = ((bf16[4,16,1,64,128]{4,3,1,2,0:T(8,128)(2,1)}), bf16[4,16,1,64,128]{4,3,1,2,0:T(8,128)(2,1)}, u32[]{:S(2)}, u32[]{:S(2)}) async-start(bf16[4,16,1,64,128]{4,3,1,2,0:T(8,128)(2,1)} %broadcast_in_dim.169), calls=%async_computation.4 | async-start | bytes 2097152 | tf_op jit(solution)/shard_map/all_to_all | solution.py:19
  170.4 6.2 %copy-start.1 = (f32[16,64,128]{2,1,0:T(8,128)S(1)}, f32[16,64,128]{2,1,0:T(8,128)}, u32[]{:S(2)}) copy-start(f32[16,64,128]{2,1,0:T(8,128)} %param.10) | copy-start | bytes 1572868
  170.4 6.2 %copy-start.3 = (f32[16,64,128]{2,1,0:T(8,128)S(1)}, f32[16,64,128]{2,1,0:T(8,128)}, u32[]{:S(2)}) copy-start(f32[16,64,128]{2,1,0:T(8,128)} %param.11) | copy-start | bytes 1572868
  170.4 6.2 %copy-start.7 = (f32[128]{0:T(128)S(1)}, f32[128]{0:T(128)}, u32[]{:S(2)}) copy-start(f32[128]{0:T(128)} %param.13) | copy-start | bytes 1540
  179.1 4.9 %collective-permute-start.8 = (bf16[4,64,128]{2,1,0:T(8,128)(2,1)S(1)}, bf16[4,64,128]{2,1,0:T(8,128)(2,1)S(1)}, u32[]{:S(2)}, u32[]{:S(2)}) collective-permute-start(bf16[4,64,128]{2,1,0:T(8,128)(2,1)S(1)} %get-tuple-element.15), channel_id=1, source_target_pairs={{1,0},{2,1},{3,2},{4,3},{5,4},{6,5},{7,6},{8,7},{9,8},{10,9},{11,1... | collective-permute-start | bytes 196616 | tf_op jit(solution)/shard_map/ppermute | solution.py:14
  181.0 5.2 %collective-permute-start.11 = (bf16[4,64,128]{2,1,0:T(8,128)(2,1)S(1)}, bf16[4,64,128]{2,1,0:T(8,128)(2,1)S(1)}, u32[]{:S(2)}, u32[]{:S(2)}) collective-permute-start(bf16[4,64,128]{2,1,0:T(8,128)(2,1)S(1)} %get-tuple-element.16), channel_id=1, source_target_pairs={{4,0},{5,1},{6,2},{7,3},{8,4},{9,5},{10,6},{11,7},{12,8},{13,9},{1... | collective-permute-start | bytes 196616 | tf_op jit(solution)/shard_map/ppermute | solution.py:14
  181.8 5.3 %collective-permute-start.10 = (bf16[4,64,128]{2,1,0:T(8,128)(2,1)S(1)}, bf16[4,64,128]{2,1,0:T(8,128)(2,1)S(1)}, u32[]{:S(2)}, u32[]{:S(2)}) collective-permute-start(bf16[4,64,128]{2,1,0:T(8,128)(2,1)S(1)} %get-tuple-element.17), channel_id=1, source_target_pairs={{3,0},{4,1},{5,2},{6,3},{7,4},{8,5},{9,6},{10,7},{11,8},{12,9},{13... | collective-permute-start | bytes 196616 | tf_op jit(solution)/shard_map/ppermute | solution.py:14
  183.1 3.9 %collective-permute-start.9 = (bf16[4,64,128]{2,1,0:T(8,128)(2,1)S(1)}, bf16[4,64,128]{2,1,0:T(8,128)(2,1)S(1)}, u32[]{:S(2)}, u32[]{:S(2)}) collective-permute-start(bf16[4,64,128]{2,1,0:T(8,128)(2,1)S(1)} %get-tuple-element.18), channel_id=1, source_target_pairs={{2,0},{3,1},{4,2},{5,3},{6,4},{7,5},{8,6},{9,7},{10,8},{11,9},{12,... | collective-permute-start | bytes 196616 | tf_op jit(solution)/shard_map/ppermute | solution.py:14
  293.5 6.1 %collective-permute-start.12 = (bf16[4,64,128]{2,1,0:T(8,128)(2,1)S(1)}, bf16[4,64,128]{2,1,0:T(8,128)(2,1)S(1)}, u32[]{:S(2)}, u32[]{:S(2)}) collective-permute-start(bf16[4,64,128]{2,1,0:T(8,128)(2,1)S(1)} %get-tuple-element.11), channel_id=1, source_target_pairs={{63,0},{0,1},{1,2},{2,3},{3,4},{4,5},{5,6},{6,7},{7,8},{8,9},{9,10... | collective-permute-start | bytes 196616 | tf_op jit(solution)/shard_map/ppermute | solution.py:14
  295.7 7.1 %collective-permute-start.15 = (bf16[4,64,128]{2,1,0:T(8,128)(2,1)S(1)}, bf16[4,64,128]{2,1,0:T(8,128)(2,1)S(1)}, u32[]{:S(2)}, u32[]{:S(2)}) collective-permute-start(bf16[4,64,128]{2,1,0:T(8,128)(2,1)S(1)} %get-tuple-element.12), channel_id=1, source_target_pairs={{60,0},{61,1},{62,2},{63,3},{0,4},{1,5},{2,6},{3,7},{4,8},{5,9},{6... | collective-permute-start | bytes 196616 | tf_op jit(solution)/shard_map/ppermute | solution.py:14
  296.7 7.9 %collective-permute-start.14 = (bf16[4,64,128]{2,1,0:T(8,128)(2,1)S(1)}, bf16[4,64,128]{2,1,0:T(8,128)(2,1)S(1)}, u32[]{:S(2)}, u32[]{:S(2)}) collective-permute-start(bf16[4,64,128]{2,1,0:T(8,128)(2,1)S(1)} %get-tuple-element.13), channel_id=1, source_target_pairs={{61,0},{62,1},{63,2},{0,3},{1,4},{2,5},{3,6},{4,7},{5,8},{6,9},{7,... | collective-permute-start | bytes 196616 | tf_op jit(solution)/shard_map/ppermute | solution.py:14
  298.4 7.3 %collective-permute-start.13 = (bf16[4,64,128]{2,1,0:T(8,128)(2,1)S(1)}, bf16[4,64,128]{2,1,0:T(8,128)(2,1)S(1)}, u32[]{:S(2)}, u32[]{:S(2)}) collective-permute-start(bf16[4,64,128]{2,1,0:T(8,128)(2,1)S(1)} %get-tuple-element.14), channel_id=1, source_target_pairs={{62,0},{63,1},{0,2},{1,3},{2,4},{3,5},{4,6},{5,7},{6,8},{7,9},{8,1... | collective-permute-start | bytes 196616 | tf_op jit(solution)/shard_map/ppermute | solution.py:14
  326.5 6.1 %copy-start.4 = (f32[16,64,128]{2,1,0:T(8,128)S(1)}, f32[16,64,128]{2,1,0:T(8,128)}, u32[]{:S(2)}) copy-start(f32[16,64,128]{2,1,0:T(8,128)} %get-tuple-element.30) | copy-start | bytes 1572868
where the time goes:
time: 336 us; the launch traced here: 334 us
  blocking collectives  179 us (53%)
  waiting for transfers between devices  41.8 us (12%)
  starting transfers between devices  37.8 us (11%)
  matrix products  26.6 us (8%)
  local copies, waits for them, and re-layouts  24.7 us (7%)
  other arithmetic  23.1 us (7%)
    all_to_all x3, blocking collectives, summed_on_arrival(): lax.all_to_all(in_blocks(value, dim, length), axis, 0, 0, tiled=True)  91.3 us
    all_to_all x5, blocking collectives, copy_for_each(): lax.all_to_all(jnp.broadcast_to(value[None], (length, *value.shape)), axi...  87.8 us
    ppermute x16, starting transfers between devices, shifted(): return lax.ppermute(block, axis, route)  30.1 us
    ppermute x16, waiting for transfers between devices, shifted(): return lax.ppermute(block, axis, route)  16.5 us
    all_to_all x1, waiting for transfers between devices, summed_on_arrival(): lax.all_to_all(in_blocks(value, dim, length), axis, 0, 0, tiled=True)  14.6 us
    dot_general x2, matrix products, shards(): jnp.dot(dosage, values, preferred_element_type=jnp.float32) * inv_scale  12.7 us
    select_n x2, other arithmetic, shards(): jnp.where(member_live[:, :, None, None], whole_grad[member_ids], zero_half)  12.3 us
    all_to_all x1, waiting for transfers between devices, copy_for_each(): lax.all_to_all(jnp.broadcast_to(value[None], (length, *value.shape)), axi...  10.7 us
  transfers between devices with their start and end apart: 18, of which 11 were waited for; matrix products, arithmetic and copies ran while one was open for 1% of the time, Pallas kernels for 0%

commit v1 on v0

v1 whole, which is shorter than its diff:
```python
import functools
import math

import jax
import jax.numpy as jnp
from jax import lax
from jax.experimental import pallas as pl
from jax.experimental.pallas import tpu as pltpu
from jax.sharding import PartitionSpec as P

MESH = pl.DeviceIdType.MESH
BF = jnp.bfloat16
F32 = jnp.float32
NZ, NX, NC = 8, 4, 2
NSAMP = 4
NVAR = 64
REACH = 4
PAIR = 4
CAP = 16
UNITS = 8
ROWS = 64
K = 128
T_CODE, T_BEGIN, T_LEN, T_SEND, T_LOCAL, T_BASE, T_COUNT, T_START = 0, 16, 32, 48, 64, 72, 76, 80


def step_kernel(
    dos_hbm, traits, cnow, cprev, bi_hbm, pen, bstart, uown,
    coef_out, res_out,
    dos, bi, coef, pb, out_v, recv_v, vals, core_out, core_in, x_out, x_in, z_out, z_in,
    rsum, gath, rbt, gfull, gs, r_in, og, out_g, recv_g, whole, tab,
    load_sem, v_s, v_r, vy_s, vy_r, c_s, c_r, x_s, x_r, z_s, z_r,
    az_s, az_r, ax_s, ax_r, ac_s, ac_r, ry_s, ry_r, g_s, g_r, w_s, w_r,
):
    s = lax.axis_index("samp")
    v = lax.axis_index("var")
    c = lax.rem(v, NC)
    x = lax.rem(v // NC, NX)
    z = v // (NC * NX)
    inv_scale = 1.0 / math.sqrt(NVAR * UNITS * 256)
    grad_scale = 0.5 / math.sqrt(NSAMP * 2048)

    def at(zz, xx, cc):
        return (s, (zz * NX + xx) * NC + cc)

    def gap(g):
        return (s, lax.rem(v + g + NVAR, NVAR))

    def samp_at(d):
        return (lax.rem(s + d, NSAMP), v)

    def x_at(d):
        return at(z, lax.rem(x + d, NX), c)

    def z_at(e):
        return at(lax.rem(z + e, NZ), x, c)

    sibling = at(z, x, 1 - c)

    def remote(src, dst, ssem, rsem, device):
        return pltpu.make_async_remote_copy(
            src_ref=src, dst_ref=dst, send_sem=ssem, recv_sem=rsem,
            device_id=device, device_id_type=MESH,
        )

    def load_rows(i, carry):
        half, rest = i // (NX * NZ), lax.rem(i, NX * NZ)
        xx, zz = rest // NZ, lax.rem(rest, NZ)
        cc = jnp.where(half == 0, 1 - c, c)
        source = ((zz * NX + xx) * NC + cc) * 32
        pltpu.make_async_copy(
            dos_hbm.at[pl.ds(pl.multiple_of(source, 32), 32)],
            dos.at[pl.ds(pl.multiple_of(i * 32, 32), 32)],
            load_sem.at[0],
        ).start()
        return carry

    prev_copy = pltpu.make_async_copy(cprev, coef.at[0], load_sem.at[1])
    now_copy = pltpu.make_async_copy(cnow, coef.at[1], load_sem.at[2])
    bi_copy = pltpu.make_async_copy(bi_hbm, bi, load_sem.at[3])
    prev_copy.start()
    now_copy.start()
    lax.fori_loop(0, NC * NX * NZ, load_rows, 0)
    bi_copy.start()

    barrier = pltpu.get_barrier_semaphore()
    peers = (
        [gap(g) for g in range(1, REACH + 1)] + [gap(-g) for g in range(1, REACH + 1)]
        + [samp_at(d) for d in range(1, NSAMP)] + [x_at(d) for d in range(1, NX)]
        + [z_at(e) for e in range(1, NZ)] + [sibling]
    )
    for peer in peers:
        pl.semaphore_signal(barrier, inc=1, device_id=peer, device_id_type=MESH)

    homes = [lax.rem(v - g + NVAR, NVAR) for g in range(1, REACH + 1)]
    counts = []
    for g in range(REACH):
        count = jnp.int32(0)
        for k in range(UNITS):
            count += (uown[homes[g] * UNITS + k] == v).astype(jnp.int32)
        counts.append(count)
    bases = []
    for g in range(REACH):
        base = jnp.int32(0)
        for other in range(REACH):
            if other != g:
                base += jnp.where(homes[other] < homes[g], counts[other], 0)
        bases.append(base)
        tab[T_BASE + g] = base
    tab[T_COUNT] = counts[0] + counts[1] + counts[2] + counts[3]
    mine = [uown[v * UNITS + k] for k in range(UNITS)]
    for k in range(UNITS):
        place = jnp.int32(0)
        for other in range(k):
            place += (mine[other] == mine[k]).astype(jnp.int32)
        ahead = mine[k] - v
        ahead = jnp.where(ahead < 0, ahead + NVAR, ahead)
        tab[T_LOCAL + k] = jnp.clip((ahead - 1) * PAIR + place, 0, CAP - 1)

    def more_tables():
        codes = [tab[T_LOCAL + k] for k in range(UNITS)]
        for code in range(CAP):
            unit = jnp.int32(0)
            for k in range(UNITS):
                unit = jnp.where(codes[k] == code, k, unit)
            tab[T_SEND + code] = unit
        for g in range(REACH):
            rank = jnp.int32(0)
            flags = [jnp.int32(1) for _ in range(PAIR)]
            for k in range(UNITS):
                at_unit = homes[g] * UNITS + k
                hit = uown[at_unit] == v
                begins = bstart[at_unit]
                for p in range(PAIR):
                    flags[p] = jnp.where(hit & (rank == p), begins, flags[p])
                rank += hit.astype(jnp.int32)
            for p in range(PAIR):
                tab[T_START + g * PAIR + p] = flags[p]
        begin = jnp.int32(0)
        starts = []
        for i in range(CAP):
            code = jnp.int32(0)
            for g in range(REACH):
                inside = (bases[g] <= i) & (i < bases[g] + counts[g])
                code = jnp.where(inside, g * PAIR + i - bases[g], code)
            code = jnp.clip(code, 0, CAP - 1)
            tab[T_CODE + i] = code
            live = i < tab[T_COUNT]
            first = (tab[T_START + code] == 1) | jnp.logical_not(live)
            starts.append(first)
            begin = jnp.where(first, i, begin)
            tab[T_BEGIN + i] = begin
        follow = jnp.int32(CAP)
        for i in reversed(range(CAP)):
            tab[T_LEN + i] = follow - tab[T_BEGIN + i]
            follow = jnp.where(starts[i], i, follow)

    prev_copy.wait()
    now_copy.wait()
    pl.semaphore_wait(barrier, len(peers))

    def tile(k, block):
        rows = dos[pl.ds(pl.multiple_of(block * 256, 256), 256), :]
        return inv_scale * jnp.dot(
            rows, vals[k].reshape(UNITS * 256, K), preferred_element_type=F32
        )

    def one_step(k, carry):
        momentum = jnp.where(k == 0, jnp.float32(0.4), jnp.float32(0.55))

        def to_point(i, carry):
            now = coef[k + 1, i]
            pb[i] = (now + momentum * (now - coef[k, i])).astype(BF)
            return carry

        lax.fori_loop(0, CAP, to_point, 0)
        sends = []
        for g in range(REACH):
            base = tab[T_BASE + g]
            for p in range(PAIR):
                out_v[k, g, p] = pb[jnp.minimum(base + p, CAP - 1)]
            copy = remote(
                out_v.at[k, g], recv_v.at[k, pl.ds(g * PAIR, PAIR)],
                v_s.at[k, g], v_r.at[k, g], gap(-(g + 1)),
            )
            copy.start()
            sends.append(copy)

        @pl.when(k == 0)
        def _():
            more_tables()

        for copy in sends:
            copy.wait_recv()
        for u in range(UNITS):
            vals[k, u, s] = recv_v[k, tab[T_LOCAL + u]]
        copies = []
        for d in (2, 1, 3):
            copy = remote(
                vals.at[k, :, s], vals.at[k, :, s], vy_s.at[k, d - 1], vy_r.at[k, d - 1], samp_at(d)
            )
            copy.start()
            copies.append(copy)
        sends += copies

        @pl.when(k == 0)
        def _():
            pltpu.make_async_copy(dos_hbm, dos, load_sem.at[0]).wait()
            bi_copy.wait()

        for copy in copies:
            copy.wait_recv()

        def core_copy(xx):
            return remote(
                core_out.at[k, xx], core_in.at[k, xx], c_s.at[k, xx], c_r.at[k, xx], sibling
            )

        def for_sibling(d, carry):
            xx = lax.rem(x + d, NX)
            core_out[k, xx] = tile(k, xx).astype(BF)
            core_copy(xx).start()
            return carry

        lax.fori_loop(1, NX + 1, for_sibling, 0)

        def x_copy(d):
            return remote(
                x_out.at[k, d - 1], x_in.at[k, d - 1], x_s.at[k, d - 1], x_r.at[k, d - 1], x_at(d)
            )

        def for_x(d, carry):
            xx = lax.rem(x + d, NX)
            mine_part = tile(k, NX + xx)
            core_copy(xx).wait_recv()
            total = mine_part + core_in[k, xx].astype(F32)

            @pl.when(d < NX)
            def _():
                x_out[k, d - 1] = total.astype(BF)
                x_copy(d).start()

            @pl.when(d == NX)
            def _():
                rsum[...] = total

            return carry

        lax.fori_loop(1, NX + 1, for_x, 0)
        for d in range(1, NX):
            x_copy(d).wait_recv()
        total = rsum[...]
        for d in range(1, NX):
            total += x_in[k, d - 1].astype(F32)
        rsum[...] = total
        z_out[k] = total.astype(BF)
        copies = []
        for e in range(1, NZ):
            there = lax.rem(z + e, NZ)
            copy = remote(
                z_out.at[k, pl.ds(pl.multiple_of(there * 32, 32), 32)], z_in.at[k, e - 1],
                z_s.at[k, e - 1], z_r.at[k, e - 1], z_at(e),
            )
            copy.start()
            copies.append(copy)
        sends += copies
        for copy in copies:
            copy.wait_recv()
        residual = rsum[pl.ds(pl.multiple_of(z * 32, 32), 32), :]
        for e in range(1, NZ):
            residual += z_in[k, e - 1].astype(F32)
        residual -= traits[...]
        res_out[...] = residual

        gath[k, 1, x, z] = residual.astype(BF)
        copies = []
        for e in range(1, NZ):
            copy = remote(
                gath.at[k, 1, x, z], gath.at[k, 1, x, z],
                az_s.at[k, e - 1], az_r.at[k, e - 1], z_at(e),
            )
            copy.start()
            copies.append(copy)
        sends += copies
        for copy in copies:
            copy.wait_recv()
        x_copies = []
        for d in (2, 1, 3):
            copy = remote(
                gath.at[k, 1, x], gath.at[k, 1, x],
                ax_s.at[k, d - 1], ax_r.at[k, d - 1], x_at(d),
            )
            copy.start()
            x_copies.append(copy)
        sends += x_copies
        last = []
        for d, arrived in ((0, None), (1, x_copies[1]), (3, x_copies[2]), (2, x_copies[0])):
            if arrived is not None:
                arrived.wait_recv()
            xx = lax.rem(x - d + NX, NX)
            copy = remote(
                gath.at[k, 1, xx], gath.at[k, 0, xx], ac_s.at[k, d], ac_r.at[k, d], sibling
            )
            copy.start()
            last.append(copy)
        sends += last
        for copy in last:
            copy.wait_recv()

        rbt[...] = gath[k].reshape(NC * NX * NZ * 32, K).astype(F32).T.astype(BF)

        def r_copy(piece, d):
            return remote(
                gs.at[k, piece, lax.rem(s + d, NSAMP)], r_in.at[k, piece, d - 1],
                ry_s.at[k, piece, d - 1], ry_r.at[k, piece, d - 1], samp_at(d),
            )

        def grad_piece(piece, carry):
            def grad_unit(uu, carry):
                first = (piece * PAIR + uu) * 256
                part = jnp.dot(
                    rbt[...], dos[:, pl.ds(pl.multiple_of(first, 256), 256)],
                    preferred_element_type=F32,
                )
                part = (grad_scale * part.T).reshape(NSAMP, ROWS, K)
                gs[k, piece, :, uu] = part.astype(BF)
                gfull[piece, uu] = part
                return carry

            lax.fori_loop(0, PAIR, grad_unit, 0)
            for d in (2, 1, 3):
                r_copy(piece, d).start()
            return carry

        lax.fori_loop(0, 2, grad_piece, 0)

        def sum_piece(piece, carry):
            for d in (1, 3, 2):
                r_copy(piece, d).wait_recv()
            for uu in range(PAIR):
                total = gfull[piece, uu, s]
                for d in range(1, NSAMP):
                    total += r_in[k, piece, d - 1, uu].astype(F32)
                og[piece * PAIR + uu] = total.astype(BF)
            return carry

        lax.fori_loop(0, 2, sum_piece, 0)
        copies = []
        for g in range(REACH):
            for p in range(PAIR):
                out_g[k, g, p] = og[tab[T_SEND + g * PAIR + p]]
            copy = remote(
                out_g.at[k, g], recv_g.at[k, pl.ds(g * PAIR, PAIR)],
                g_s.at[k, g], g_r.at[k, g], gap(g + 1),
            )
            copy.start()
            copies.append(copy)
        sends += copies
        for copy in copies:
            copy.wait_recv()
        for i in range(CAP):
            whole[k, i, s] = recv_g[k, tab[T_CODE + i]]
        copies = []
        for d in (2, 1, 3):
            copy = remote(
                whole.at[k, :, s], whole.at[k, :, s], w_s.at[k, d - 1], w_r.at[k, d - 1], samp_at(d)
            )
            copy.start()
            copies.append(copy)
        sends += copies
        for copy in copies:
            copy.wait_recv()

        def update(i, carry):
            begin, length = tab[T_BEGIN + i], tab[T_LEN + i]
            direction = jnp.zeros((ROWS, K), F32)
            for q in range(PAIR):
                member = whole[k, jnp.clip(begin + q, 0, CAP - 1)].reshape(256, K)
                part = jnp.dot(
                    bi[i, :, q * 256 : (q + 1) * 256], member, preferred_element_type=F32
                )
                direction += jnp.where(q < length, part, 0.0)
            now = coef[k + 1, i]
            stepped = now + momentum * (now - coef[k, i]) - direction
            level = pen[...]
            updated = stepped - jnp.clip(stepped, -level, level)
            updated = jnp.where(i < tab[T_COUNT], updated, 0.0)
            coef[k + 2, i] = updated
            coef_out[i] = updated
            return carry

        lax.fori_loop(0, CAP, update, 0)
        for copy in sends:
            copy.wait_send()
        for xx in range(NX):
            core_copy(xx).wait_send()
        for d in range(1, NX):
            x_copy(d).wait_send()
        for piece in range(2):
            for d in range(1, NSAMP):
                r_copy(piece, d).wait_send()
        return carry

    lax.fori_loop(0, 2, one_step, 0)


def shards(dosage, traits, coef_now, coef_prev, block_inverse, penalty, block_start, unit_owner):
    panel = block_inverse.reshape(CAP, ROWS, PAIR * 256)
    vmem = pl.BlockSpec(memory_space=pltpu.VMEM)
    smem = pl.BlockSpec(memory_space=pltpu.SMEM)
    anywhere = pl.BlockSpec(memory_space=pl.ANY)
    dma = pltpu.SemaphoreType.DMA
    pairs = []
    for count in (REACH, 3, NX, 3, 7, 7, 3, NX):
        pairs += [dma((2, count))] * 2
    pairs += [dma((2, 2, 3))] * 2
    for count in (REACH, 3):
        pairs += [dma((2, count))] * 2
    return pl.pallas_call(
        step_kernel,
        out_shape=(
            jax.ShapeDtypeStruct((CAP, ROWS, K), F32),
            jax.ShapeDtypeStruct((32, K), F32),
        ),
        in_specs=[anywhere, vmem, anywhere, anywhere, anywhere, vmem, smem, smem],
        out_specs=(vmem, vmem),
        scratch_shapes=[
            pltpu.VMEM((2048, 2048), BF),
            pltpu.VMEM((CAP, ROWS, 1024), BF),
            pltpu.VMEM((4, CAP, ROWS, K), F32),
            pltpu.VMEM((CAP, ROWS, K), BF),
            pltpu.VMEM((2, REACH, PAIR, ROWS, K), BF),
            pltpu.VMEM((2, CAP, ROWS, K), BF),
            pltpu.VMEM((2, UNITS, NSAMP, ROWS, K), BF),
            pltpu.VMEM((2, NX, 256, K), BF),
            pltpu.VMEM((2, NX, 256, K), BF),
            pltpu.VMEM((2, 3, 256, K), BF),
            pltpu.VMEM((2, 3, 256, K), BF),
            pltpu.VMEM((2, 256, K), BF),
            pltpu.VMEM((2, 7, 32, K), BF),
            pltpu.VMEM((256, K), F32),
            pltpu.VMEM((2, NC, NX, NZ, 32, K), BF),
            pltpu.VMEM((K, 2048), BF),
            pltpu.VMEM((2, PAIR, NSAMP, ROWS, K), F32),
            pltpu.VMEM((2, 2, NSAMP, PAIR, ROWS, K), BF),
            pltpu.VMEM((2, 2, 3, PAIR, ROWS, K), BF),
            pltpu.VMEM((UNITS, ROWS, K), BF),
            pltpu.VMEM((2, REACH, PAIR, ROWS, K), BF),
            pltpu.VMEM((2, CAP, ROWS, K), BF),
            pltpu.VMEM((2, CAP, NSAMP, ROWS, K), BF),
            pltpu.SMEM((96,), jnp.int32),
            dma((4,)),
            *pairs,
        ],
        compiler_params=pltpu.CompilerParams(
            collective_id=0, has_side_effects=True, vmem_limit_bytes=48 * 1024 * 1024
        ),
    )(
        dosage, traits, coef_now, coef_prev, panel, penalty.reshape(1, K), block_start, unit_owner
    )


def solution(mesh):
    placed = (
        P("samp", "var"),
        P(("samp", "var"), None),
        P("var", "samp", None),
        P("var", "samp", None),
        P("var", "samp", None, None),
        P(),
        P(),
        P(),
    )
    return jax.shard_map(
        shards,
        mesh=mesh,
        in_specs=placed,
        out_specs=(P("var", "samp", None), P(("samp", "var"), None)),
        check_vma=False,
    )
```

time: 336 us -> 163 us (0.49)
  blocking collectives: 179 us -> 0 us
  Pallas kernels: 0 us -> 157 us
  waiting for transfers between devices: 41.8 us -> 0 us
  starting transfers between devices: 37.8 us -> 0 us
  matrix products: 26.6 us -> 0 us
  other arithmetic: 23.1 us -> 0 us
  local copies, waits for them, and re-layouts: 24.7 us -> 4.74 us
    all_to_all x8 -> x0, blocking collectives: 179 us -> none  [the longest x3 91.3 us: summed_on_arrival(): lax.all_to_all(in_blocks(value, dim, length), axis, 0, 0, tiled=True)]
    pallas_call x0 -> x1, Pallas kernels: none -> 157 us  [shards(): pl.pallas_call(step_kernel, out_shape=(jax.ShapeDtypeStruct((CAP, ROWS, K...]
    ppermute x16 -> x0, starting transfers between devices: 30.1 us -> none  [shifted(): return lax.ppermute(block, axis, route)]
    dot_general x6 -> x0, matrix products: 26.6 us -> none  [the longest x2 12.7 us: shards(): jnp.dot(dosage, values, preferred_element_type=jnp.float32) * inv_scale]
    all_to_all x2 -> x0, waiting for transfers between devices: 25.3 us -> none  [the longest x1 14.6 us: summed_on_arrival(): lax.all_to_all(in_blocks(value, dim, length), axis, 0, 0, tiled=True)]
    ppermute x16 -> x0, waiting for transfers between devices: 16.5 us -> none  [shifted(): return lax.ppermute(block, axis, route)]
    select_n x15 -> x0, other arithmetic: 12.9 us -> none  [the longest x2 12.3 us: shards(): jnp.where(member_live[:, :, None, None], whole_grad[member_ids], zero_half)]
    gather x12 -> x0, local copies, waits for them, and re-layouts: 12.4 us -> none  [the longest x2 6.02 us: shards(): whole_grad[member_ids]]
  transfers between devices with their start and end apart: 18 -> 0, of which waited for: 11 -> 0; matrix products, arithmetic and copies ran while one was open for 1% -> 0% of each run, Pallas kernels for 0% -> 0%
where the time goes in v1:
time: 163 us
  Pallas kernels  157 us (96%)
  local copies, waits for them, and re-layouts  4.74 us (3%)
    pallas_call x1, Pallas kernels, shards(): pl.pallas_call(step_kernel, out_shape=(jax.ShapeDtypeStruct((CAP, ROWS, K...  157 us
    reshape x1, local copies, waits for them, and re-layouts, shards(): panel = block_inverse.reshape(CAP, ROWS, PAIR * 256)  3.31 us

profile of v1, /device:TPU:1, one launch (start us, length us, event | category | flops | bytes accessed | tf_op | source)
XLA Modules:
  0.0 163.0 jit_solution(6121362908095140885)
XLA Ops:
  0.6 0.0 copy-start
  0.6 0.0 copy-start.1
  0.7 0.0 copy-start.2
  0.7 0.0 copy-start.3
  0.7 0.0 copy-start.4
  0.7 0.0 copy-start.5
  0.7 3.3 %reshape.10.bi_hbm = bf16[16,64,1024]{2,1,0:T(8,128)(2,1)S(1)} reshape(bf16[16,64,4,256]{3,2,1,0:T(4,128)(2,1)} %param.12) | data formatting | bytes 4194304 | tf_op jit(solution)/shard_map/reshape | solution.py:407
  4.0 0.0 copy-done
  4.0 0.0 copy-done.1
  4.0 0.0 copy-done.2
  4.0 0.0 copy-done.3
  4.1 0.0 copy-done.4
  4.1 0.0 copy-done.5
  4.1 157.5 %shard_map.95 = (f32[16,64,128]{2,1,0:T(8,128)S(1)}, f32[32,128]{1,0:T(8,128)S(1)}) custom-call(bf16[2048,2048]{1,0:T(8,128)(2,1)} %dos_hbm.1, f32[32,128]{1,0:T(8,128)S(1)} %copy-done.2, f32[16,64,128]{2,1,0:T(8,128)S(1)} %copy-done, f32[16,64,128]{2,1,0:T(8,128)S(1)} %copy-done.1, bf16[16,64,1024]{2,1,0:T(8,128)(2,1)S(1)} %reshape.10.bi_hbm, ...), custom_call_target="tpu_custom_call" | custom-call | tf_op jit(solution)/shard_map/pallas_call | solution.py:418
  161.6 0.8 copy.12
  162.4 0.6 copy.13
Async XLA Ops:
  0.6 3.4 %copy-start = (f32[16,64,128]{2,1,0:T(8,128)S(1)}, f32[16,64,128]{2,1,0:T(8,128)}, u32[]{:S(2)}) copy-start(f32[16,64,128]{2,1,0:T(8,128)} %cnow.1) | copy-start | bytes 1572868
  0.6 3.4 %copy-start.1 = (f32[16,64,128]{2,1,0:T(8,128)S(1)}, f32[16,64,128]{2,1,0:T(8,128)}, u32[]{:S(2)}) copy-start(f32[16,64,128]{2,1,0:T(8,128)} %cprev.1) | copy-start | bytes 1572868
  0.7 3.4 %copy-start.2 = (f32[32,128]{1,0:T(8,128)S(1)}, f32[32,128]{1,0:T(8,128)}, u32[]{:S(2)}) copy-start(f32[32,128]{1,0:T(8,128)} %traits.1) | copy-start | bytes 49156
  0.7 3.4 %copy-start.3 = (s32[512]{0:T(512)S(1)}, s32[512]{0:T(512)}, u32[]{:S(2)}) copy-start(s32[512]{0:T(512)} %bstart.1) | copy-start | bytes 6148
  0.7 3.4 %copy-start.4 = (s32[512]{0:T(512)S(1)}, s32[512]{0:T(512)}, u32[]{:S(2)}) copy-start(s32[512]{0:T(512)} %uown.1) | copy-start | bytes 6148
  0.7 3.4 %copy-start.5 = (f32[128]{0:T(128)S(1)}, f32[128]{0:T(128)}, u32[]{:S(2)}) copy-start(f32[128]{0:T(128)} %param.13) | copy-start | bytes 1540

commit v2 on v1

v2 whole, which is shorter than its diff:
```python
import functools
import math

import jax
import jax.numpy as jnp
from jax import lax
from jax.experimental import pallas as pl
from jax.experimental.pallas import tpu as pltpu
from jax.sharding import PartitionSpec as P

MESH = pl.DeviceIdType.MESH
BF = jnp.bfloat16
F32 = jnp.float32
NZ, NX, NC = 8, 4, 2
NSAMP = 4
NVAR = 64
REACH = 4
PAIR = 4
CAP = 16
UNITS = 8
ROWS = 64
K = 128
T_CODE, T_BEGIN, T_LEN, T_SEND, T_SLOT, T_LOCAL, T_COUNT = 0, 16, 32, 48, 64, 80, 88
MOMENTA = (0.4, 0.55)


def step_kernel(
    dos_hbm, traits, cnow, cprev, bi, pen, bstart, uown,
    coef_out, res_out,
    dos, panel, coef, point, out_v, recv_v, vals, core_out, core_in, x_out, x_in, z_out, z_in,
    part, rsum, gath, rbt, gfull, gs, r_in, og, out_g, whole, tab,
    load_sem, v_s, v_r, vy_s, vy_r, c_s, c_r, x_s, x_r, z_s, z_r,
    az_s, az_r, ax_s, ax_r, ac_s, ac_r, ry_s, ry_r, g_s, g_r, w_s, w_r, f_s, f_r,
):
    s = lax.axis_index("samp")
    v = lax.axis_index("var")
    c = lax.rem(v, NC)
    x = lax.rem(v // NC, NX)
    z = v // (NC * NX)
    inv_scale = 1.0 / math.sqrt(NVAR * UNITS * 256)
    grad_scale = 0.5 / math.sqrt(NSAMP * 2048)

    def at(zz, xx, cc):
        return (s, (zz * NX + xx) * NC + cc)

    gaps = {g: (s, lax.rem(v + g + NVAR, NVAR)) for g in range(-REACH, REACH + 1)}
    samps = [lax.rem(s + d, NSAMP) for d in range(NSAMP)]
    xs = [lax.rem(x + d, NX) for d in range(NX)]
    zs = [lax.rem(z + e, NZ) for e in range(NZ)]
    halves = [z // 4 * 4, (1 - z // 4) * 4]
    samp_at = [(samps[d], v) for d in range(NSAMP)]
    x_at = [at(z, xs[d], c) for d in range(NX)]
    z_at = [at(zs[e], x, c) for e in range(NZ)]
    half_at = [[at(halves[half] + lax.rem(z + j, 4), x, c) for j in range(4)] for half in range(2)]

    sibling = at(z, x, 1 - c)

    def remote(src, dst, ssem, rsem, device):
        return pltpu.make_async_remote_copy(
            src_ref=src, dst_ref=dst, send_sem=ssem, recv_sem=rsem,
            device_id=device, device_id_type=MESH,
        )

    def wait_arrived(ref, sem):
        remote(ref, ref, sem, sem, sibling).wait_recv()

    def wait_sent(ref, sem):
        remote(ref, ref, sem, sem, sibling).wait_send()

    load_copies = [
        pltpu.make_async_copy(
            dos_hbm.at[:, xx, cc], dos.at[half, xx], load_sem.at[half * NX + xx]
        )
        for half, cc in ((0, 1 - c), (1, c))
        for xx in range(NX)
    ]

    barrier = pltpu.get_barrier_semaphore()
    peers = (
        [gaps[g] for g in range(-REACH, REACH + 1) if g != 0]
        + samp_at[1:] + x_at[1:] + z_at[1:] + [sibling]
    )
    for peer in peers:
        pl.semaphore_signal(barrier, inc=1, device_id=peer, device_id_type=MESH)

    homes = [gaps[-g][1] for g in range(1, REACH + 1)]
    counts = []
    for g in range(REACH):
        count = jnp.int32(0)
        for k in range(UNITS):
            count += (uown[homes[g] * UNITS + k] == v).astype(jnp.int32)
        counts.append(count)
    bases = []
    for g in range(REACH):
        base = jnp.int32(0)
        for other in range(REACH):
            if other != g:
                base += jnp.where(homes[other] < homes[g], counts[other], 0)
        bases.append(base)
        for p in range(PAIR):
            tab[T_SLOT + g * PAIR + p] = jnp.minimum(base + p, CAP - 1)
    tab[T_COUNT] = counts[0] + counts[1] + counts[2] + counts[3]

    def more_tables():
        mine = [uown[v * UNITS + k] for k in range(UNITS)]
        codes = []
        for k in range(UNITS):
            place = jnp.int32(0)
            for other in range(k):
                place += (mine[other] == mine[k]).astype(jnp.int32)
            ahead = mine[k] - v
            ahead = jnp.where(ahead < 0, ahead + NVAR, ahead)
            codes.append(jnp.clip((ahead - 1) * PAIR + place, 0, CAP - 1))
            tab[T_LOCAL + k] = codes[k]
        for code in range(CAP):
            unit = jnp.int32(0)
            for k in range(UNITS):
                unit = jnp.where(codes[k] == code, k, unit)
            tab[T_SEND + code] = unit
        for g in range(REACH):
            rank = jnp.int32(0)
            flags = [jnp.int32(1) for _ in range(PAIR)]
            for k in range(UNITS):
                at_unit = homes[g] * UNITS + k
                hit = uown[at_unit] == v
                begins = bstart[at_unit]
                for p in range(PAIR):
                    flags[p] = jnp.where(hit & (rank == p), begins, flags[p])
                rank += hit.astype(jnp.int32)
            begin = jnp.int32(0)
            begin_of = []
            for p in range(PAIR):
                begin = jnp.where(flags[p] == 1, p, begin)
                begin_of.append(begin)
                tab[T_BEGIN + g * PAIR + p] = begin
            follow = jnp.int32(PAIR)
            for p in reversed(range(PAIR)):
                tab[T_LEN + g * PAIR + p] = follow - begin_of[p]
                follow = jnp.where(flags[p] == 1, p, follow)
        for i in range(CAP):
            code = jnp.int32(0)
            for g in range(REACH):
                inside = (bases[g] <= i) & (i < bases[g] + counts[g])
                code = jnp.where(inside, g * PAIR + i - bases[g], code)
            tab[T_CODE + i] = jnp.clip(code, 0, CAP - 1)

    def v_copy(k, g):
        here = pl.ds(g * PAIR, PAIR)
        return remote(
            out_v.at[k, here], recv_v.at[k, here], v_s.at[k], v_r.at[k], gaps[-(g + 1)]
        )

    for code in range(CAP):
        slot = tab[T_SLOT + code]
        now, before = cnow[slot], cprev[slot]
        coef[code] = now
        moved = now + MOMENTA[0] * (now - before)
        point[code] = moved
        out_v[0, code] = moved.astype(BF)
    pl.semaphore_wait(barrier, len(peers))
    for g in reversed(range(REACH)):
        v_copy(0, g).start()
    for copy in load_copies:
        copy.start()
    more_tables()

    def fill_panel(code, carry):
        slot, begin, length = tab[T_SLOT + code], tab[T_BEGIN + code], tab[T_LEN + code]
        for member in range(PAIR):
            q = member - begin
            block = bi[slot, jnp.clip(q, 0, PAIR - 1)]
            live = (q >= 0) & (q < length)
            panel[code, :, member * 256 : (member + 1) * 256] = jnp.where(live, block, zero)
        return carry

    zero = jnp.zeros((), BF)
    lax.fori_loop(0, CAP, fill_panel, 0)

    def product(k, block, half):
        columns = slice(half * 1024, (half + 1) * 1024)
        return jnp.dot(
            dos[block // NX, lax.rem(block, NX), :, :, columns].reshape(256, 1024),
            vals[k, half * PAIR : (half + 1) * PAIR].reshape(1024, K),
            preferred_element_type=F32,
        )

    def tile(k, block):
        return inv_scale * (part[block] + product(k, block, 1))

    def one_step(k, carry):
        wait_arrived(recv_v.at[k], v_r.at[k])
        for u in range(UNITS):
            vals[k, u, s] = recv_v[k, tab[T_LOCAL + u]]
        for half in range(2):
            here = vals.at[k, pl.ds(half * PAIR, PAIR), s]
            for d in (2, 1, 3):
                remote(here, here, vy_s.at[k], vy_r.at[k, half], samp_at[d]).start()

        @pl.when(k == 0)
        def _():
            for copy in load_copies:
                copy.wait()

        wait_arrived(x_in.at[k], vy_r.at[k, 0])

        def first_half(block, carry):
            part[block] = product(k, block, 0)
            return carry

        lax.fori_loop(0, 2 * NX, first_half, 0)
        wait_arrived(x_in.at[k], vy_r.at[k, 1])

        def core_copy(xx):
            return remote(
                core_out.at[k, xx], core_in.at[k, xx], c_s.at[k], c_r.at[k, xx], sibling
            )

        for d in (2, 1, 3, 0):
            core_out[k, xs[d]] = tile(k, xs[d]).astype(BF)
            core_copy(xs[d]).start()
        for d in (2, 1, 3, 0):
            mine_part = tile(k, NX + xs[d])
            core_copy(xs[d]).wait_recv()
            total = mine_part + core_in[k, xs[d]].astype(F32)
            if d:
                x_out[k, d - 1] = total.astype(BF)
                remote(
                    x_out.at[k, d - 1], x_in.at[k, d - 1], x_s.at[k], x_r.at[k], x_at[d]
                ).start()
        wait_arrived(x_in.at[k], x_r.at[k])
        for d in range(1, NX):
            total += x_in[k, d - 1].astype(F32)
        rsum[...] = total
        z_out[k] = total.astype(BF)
        for e in (4, 3, 5, 2, 6, 1, 7):
            there = pl.ds(pl.multiple_of(zs[e] * 32, 32), 32)
            remote(
                z_out.at[k, there], z_in.at[k, e - 1], z_s.at[k], z_r.at[k], z_at[e]
            ).start()
        residual = rsum[pl.ds(pl.multiple_of(z * 32, 32), 32), :] - traits[...]
        wait_arrived(z_in.at[k], z_r.at[k])
        for e in range(1, NZ):
            residual += z_in[k, e - 1].astype(F32)
        res_out[...] = residual

        gath[k, 1, x, z] = residual.astype(BF)
        mine_rows = gath.at[k, 1, x, z]
        for half, j in ((1, 0), (1, 1), (1, 3), (1, 2), (0, 2), (0, 1), (0, 3)):
            remote(
                mine_rows, mine_rows, az_s.at[k], az_r.at[k, half], half_at[half][j]
            ).start()

        def gath_x(half, d):
            here = gath.at[k, 1, x, pl.ds(halves[half], 4)]
            return remote(here, here, ax_s.at[k], ax_r.at[k, half, d], x_at[d])

        def gath_core(half, d):
            xx, here = xs[NX - d if d else 0], pl.ds(halves[half], 4)
            return remote(
                gath.at[k, 1, xx, here], gath.at[k, 0, xx, here], ac_s.at[k], ac_r.at[k], sibling
            )

        for half in range(2):
            wait_arrived(z_in.at[k, pl.ds(0, 3 + half)], az_r.at[k, half])
            for d in (2, 1, 3):
                gath_x(half, d).start()
            gath_core(half, 0).start()
        for half in range(2):
            for d in (1, 3, 2):
                gath_x(half, d).wait_recv()
                gath_core(half, d).start()
        wait_arrived(gath.at[k, 0], ac_r.at[k])

        rbt[...] = gath[k].reshape(NC * NX * NZ * 32, K).astype(F32).T.astype(BF)

        def grad_piece(piece, carry):
            def grad_unit(uu, carry):
                first = (piece * PAIR + uu) * 256
                grad = jnp.dot(
                    rbt[...],
                    dos[:, :, :, :, pl.ds(pl.multiple_of(first, 256), 256)].reshape(2048, 256),
                    preferred_element_type=F32,
                )
                grad = (grad_scale * grad.T).reshape(NSAMP, ROWS, K)
                gs[k, piece, :, uu] = grad.astype(BF)
                gfull[piece, uu] = grad
                return carry

            lax.fori_loop(0, PAIR, grad_unit, 0)
            for d in (2, 1, 3):
                remote(
                    gs.at[k, piece, samps[d]], r_in.at[k, piece, d - 1],
                    ry_s.at[k], ry_r.at[k, piece], samp_at[d],
                ).start()
            return carry

        lax.fori_loop(0, 2, grad_piece, 0)
        for piece in range(2):
            wait_arrived(r_in.at[k, piece], ry_r.at[k, piece])
            for uu in range(PAIR):
                total = gfull[piece, uu, s]
                for d in range(1, NSAMP):
                    total += r_in[k, piece, d - 1, uu].astype(F32)
                og[piece * PAIR + uu] = total.astype(BF)

        def g_copy(g):
            here = pl.ds(g * PAIR, PAIR)
            return remote(
                out_g.at[k, here], whole.at[k, here, s], g_s.at[k], g_r.at[k, g], gaps[g + 1]
            )

        for g in reversed(range(REACH)):
            for p in range(PAIR):
                out_g[k, g * PAIR + p] = og[tab[T_SEND + g * PAIR + p]]
            g_copy(g).start()
        for g in range(REACH):
            g_copy(g).wait_recv()
            here = whole.at[k, pl.ds(g * PAIR, PAIR), s]
            for d in (1, 3):
                remote(here, here, w_s.at[k], w_r.at[k, g], samp_at[d]).start()
        for g in range(REACH):
            wait_arrived(out_g.at[k, pl.ds(0, 2 * PAIR)], w_r.at[k, g])
            for d, first in ((1, 0), (3, PAIR // 2)):
                here = whole.at[k, pl.ds(g * PAIR + first, PAIR // 2), samps[NSAMP - d]]
                remote(here, here, f_s.at[k], f_r.at[k, g], samp_at[d]).start()

        level = pen[...]
        for g in range(REACH):
            wait_arrived(out_g.at[k, pl.ds(0, PAIR)], f_r.at[k, g])
            here = pl.ds(g * PAIR, PAIR)
            directions = jnp.dot(
                panel[here].reshape(PAIR * ROWS, PAIR * 256),
                whole[k, here].reshape(PAIR * 256, K),
                preferred_element_type=F32,
            ).reshape(PAIR, ROWS, K)
            for p in range(PAIR):
                code = g * PAIR + p
                stepped = point[code] - directions[p]
                updated = stepped - jnp.clip(stepped, -level, level)
                moved = updated + MOMENTA[1] * (updated - coef[code])
                coef[code] = updated
                point[code] = moved
                out_v[k + 1, code] = moved.astype(BF)

            @pl.when(k == 0)
            def _():
                v_copy(1, g).start()

        return carry

    lax.fori_loop(0, 2, one_step, 0)
    for i in range(CAP):
        coef_out[i] = jnp.where(i < tab[T_COUNT], coef[tab[T_CODE + i]], 0.0)
    for k in range(2):
        for ref, sem in (
            (recv_v, v_s), (r_in, vy_s), (core_out, c_s), (x_out, x_s), (z_in, z_s), (z_in, az_s),
            (x_out, ax_s), (core_out, ac_s), (r_in, ry_s), (out_g, g_s), (vals, w_s), (out_g, f_s),
        ):
            wait_sent(ref.at[k], sem.at[k])


def shards(dosage, traits, coef_now, coef_prev, block_inverse, penalty, block_start, unit_owner):
    panel = block_inverse.transpose(0, 2, 1, 3)
    vmem = pl.BlockSpec(memory_space=pltpu.VMEM)
    smem = pl.BlockSpec(memory_space=pltpu.SMEM)
    anywhere = pl.BlockSpec(memory_space=pl.ANY)
    dma = pltpu.SemaphoreType.DMA
    pairs = []
    for arrivals in (
        (2,), (2, 2), (2, NX), (2,), (2,), (2, 2), (2, 2, NX), (2,), (2, 2), (2, REACH),
        (2, REACH), (2, REACH),
    ):
        pairs += [dma((2,)), dma(arrivals)]
    return pl.pallas_call(
        step_kernel,
        out_shape=(
            jax.ShapeDtypeStruct((CAP, ROWS, K), F32),
            jax.ShapeDtypeStruct((32, K), F32),
        ),
        in_specs=[anywhere, vmem, vmem, vmem, vmem, vmem, smem, smem],
        out_specs=(vmem, vmem),
        scratch_shapes=[
            pltpu.VMEM((NC, NX, NZ, 32, 2048), BF),
            pltpu.VMEM((CAP, ROWS, PAIR * 256), BF),
            pltpu.VMEM((CAP, ROWS, K), F32),
            pltpu.VMEM((CAP, ROWS, K), F32),
            pltpu.VMEM((3, CAP, ROWS, K), BF),
            pltpu.VMEM((2, CAP, ROWS, K), BF),
            pltpu.VMEM((2, UNITS, NSAMP, ROWS, K), BF),
            pltpu.VMEM((2, NX, 256, K), BF),
            pltpu.VMEM((2, NX, 256, K), BF),
            pltpu.VMEM((2, 3, 256, K), BF),
            pltpu.VMEM((2, 3, 256, K), BF),
            pltpu.VMEM((2, 256, K), BF),
            pltpu.VMEM((2, 7, 32, K), BF),
            pltpu.VMEM((NC * NX, 256, K), F32),
            pltpu.VMEM((256, K), F32),
            pltpu.VMEM((2, NC, NX, NZ, 32, K), BF),
            pltpu.VMEM((K, 2048), BF),
            pltpu.VMEM((2, PAIR, NSAMP, ROWS, K), F32),
            pltpu.VMEM((2, 2, NSAMP, PAIR, ROWS, K), BF),
            pltpu.VMEM((2, 2, 3, PAIR, ROWS, K), BF),
            pltpu.VMEM((UNITS, ROWS, K), BF),
            pltpu.VMEM((2, CAP, ROWS, K), BF),
            pltpu.VMEM((2, CAP, NSAMP, ROWS, K), BF),
            pltpu.SMEM((96,), jnp.int32),
            dma((8,)),
            *pairs,
        ],
        compiler_params=pltpu.CompilerParams(
            collective_id=0, has_side_effects=True, vmem_limit_bytes=48 * 1024 * 1024
        ),
    )(
        dosage.reshape(NZ, NX, NC, 32, UNITS * 256), traits, coef_now, coef_prev, panel, penalty.reshape(1, K), block_start, unit_owner
    )


def solution(mesh):
    placed = (
        P("samp", "var"),
        P(("samp", "var"), None),
        P("var", "samp", None),
        P("var", "samp", None),
        P("var", "samp", None, None),
        P(),
        P(),
        P(),
    )
    return jax.shard_map(
        shards,
        mesh=mesh,
        in_specs=placed,
        out_specs=(P("var", "samp", None), P(("samp", "var"), None)),
        check_vma=False,
    )
```

time: 163 us -> 143 us (0.88)
  Pallas kernels: 157 us -> 137 us
    pallas_call x1, Pallas kernels: 157 us -> 137 us  [shards(): pl.pallas_call(step_kernel, out_shape=(jax.ShapeDtypeStruct((CAP, ROWS, K...]
    reshape x1 -> x0, local copies, waits for them, and re-layouts: 3.31 us -> none  [shards(): panel = block_inverse.reshape(CAP, ROWS, PAIR * 256)]
    unnamed x14 -> x15, local copies, waits for them, and re-layouts: 1.43 us -> 3.51 us
where the time goes in v2:
time: 143 us; the launch traced here: 141 us
  Pallas kernels  137 us (96%)
  local copies, waits for them, and re-layouts  3.51 us (2%)
    pallas_call x1, Pallas kernels, shards(): pl.pallas_call(step_kernel, out_shape=(jax.ShapeDtypeStruct((CAP, ROWS, K...  137 us
    unnamed x15, local copies, waits for them, and re-layouts  3.51 us

profile of v2, /device:TPU:1, one launch (start us, length us, event | category | flops | bytes accessed | tf_op | source)
XLA Modules:
  0.0 141.4 jit_solution(8137520712048840357)
XLA Ops:
  0.6 0.0 copy-start
  0.6 0.0 copy-start.1
  0.7 0.0 copy-start.2
  0.7 0.0 copy-start.3
  0.7 0.0 copy-start.4
  0.7 0.0 copy-start.5
  0.7 2.1 %copy.12 = bf16[16,64,4,256]{3,1,2,0:T(8,128)(2,1)S(1)} copy(bf16[16,64,4,256]{3,2,1,0:T(4,128)(2,1)} %param.12) | data formatting | bytes 4194304 | tf_op args[4]
  2.8 0.0 copy-done
  2.8 0.0 copy-done.1
  2.8 0.0 copy-done.2
  2.8 0.0 copy-done.3
  2.8 0.0 copy-done.4
  2.8 0.0 copy-done.5
  2.8 137.2 %shard_map.95 = (f32[16,64,128]{2,1,0:T(8,128)S(1)}, f32[32,128]{1,0:T(8,128)S(1)}) custom-call(bf16[8,4,2,32,2048]{4,3,2,1,0:T(8,128)(2,1)} %bitcast.7, f32[32,128]{1,0:T(8,128)S(1)} %copy-done.2, f32[16,64,128]{2,1,0:T(8,128)S(1)} %copy-done, f32[16,64,128]{2,1,0:T(8,128)S(1)} %copy-done.1, bf16[16,4,64,256]{3,2,1,0:T(8,128)(2,1)S(1)} %bitcast.5, ...), custom_call_target="tpu_custom_call" | custom-call | tf_op jit(solution)/shard_map/pallas_call | solution.py:374
  140.0 0.8 copy.15
  140.8 0.6 copy.16
Async XLA Ops:
  0.6 2.2 %copy-start = (f32[16,64,128]{2,1,0:T(8,128)S(1)}, f32[16,64,128]{2,1,0:T(8,128)}, u32[]{:S(2)}) copy-start(f32[16,64,128]{2,1,0:T(8,128)} %cnow.1) | copy-start | bytes 1572868
  0.6 2.2 %copy-start.1 = (f32[16,64,128]{2,1,0:T(8,128)S(1)}, f32[16,64,128]{2,1,0:T(8,128)}, u32[]{:S(2)}) copy-start(f32[16,64,128]{2,1,0:T(8,128)} %cprev.1) | copy-start | bytes 1572868
  0.7 2.2 %copy-start.2 = (f32[32,128]{1,0:T(8,128)S(1)}, f32[32,128]{1,0:T(8,128)}, u32[]{:S(2)}) copy-start(f32[32,128]{1,0:T(8,128)} %traits.1) | copy-start | bytes 49156
  0.7 2.2 %copy-start.3 = (s32[512]{0:T(512)S(1)}, s32[512]{0:T(512)}, u32[]{:S(2)}) copy-start(s32[512]{0:T(512)} %bstart.1) | copy-start | bytes 6148
  0.7 2.2 %copy-start.4 = (s32[512]{0:T(512)S(1)}, s32[512]{0:T(512)}, u32[]{:S(2)}) copy-start(s32[512]{0:T(512)} %uown.1) | copy-start | bytes 6148
  0.7 2.2 %copy-start.5 = (f32[128]{0:T(128)S(1)}, f32[128]{0:T(128)}, u32[]{:S(2)}) copy-start(f32[128]{0:T(128)} %param.13) | copy-start | bytes 1540
